TPU v7x, 256 devices: a whole 4x4x8 slice. The times are simulated.
256 devices in a mesh: gx: 8 (over z_lo, x), gy: 32 (over z_hi, y, core).
Axes of the slice: x: 4, y: 4, z: 8 (z_hi: 4, z_lo: 2; z = z_hi * 2 + z_lo), core: 2. Of those that a mesh axis runs over, the one named last changes fastest.
Arguments:
- vectors: bfloat16 [65536, 32, 128], P(('gx', 'gy')), may hold values from -6 to 6
- coupling_table: bfloat16 [8, 16, 128, 128], replicated, may hold values from -0.375 to 0.375
- factor_index: int32 [65536, 8, 2], P(('gx', 'gy')), may hold values from 0 to 15
- level_order: int32 [8], replicated, may hold values from 0 to 7, each once
Outputs:
- applied: bfloat16 [65536, 32, 128], P(('gx', 'gy'))
Inputs may be any that keep to these rules, and one draw needn't show every extreme that they name: `factor_index`: table entries of the coupling matrices. `level_order`: each level slot appears once.
All inputs are finite; a program needn't handle non-finite values.
Results may differ from a plain program's by a relative error of at most 0.0086.
Values may be sent and summed in bfloat16 or wider, within the bound.
A program may use at most 64 MiB of HBM per device.

v0:
```python
import math

import jax
import jax.numpy as jnp
from jax import lax
from jax.sharding import PartitionSpec as P


def partner_2(array, axis, distance):
    return lax.ppermute(array, axis, [(i, i ^ 1 << distance) for i in range(lax.axis_size(axis))])


def body(vectors, coupling_table, factor_index, level_order):
    middle_bits = lax.axis_size("gy").bit_length() - 1
    high_bits = lax.axis_size("gx").bit_length() - 1

    def apply_level(field, partner, indices, position):
        level_slot = level_order[position]
        level_table = lax.dynamic_index_in_dim(coupling_table, level_slot, 0, keepdims=False)
        chosen = lax.dynamic_index_in_dim(indices, level_slot, 1, keepdims=False)
        block_total = field.shape[0]
        group_size = math.gcd(block_total, 64)
        group_total = block_total // group_size

        def one_group(operands):
            own_blocks, other_blocks, selected = operands
            first = jnp.take(level_table, selected[:, 0], axis=0)
            second = jnp.take(level_table, selected[:, 1], axis=0)
            local_part = jnp.einsum(
                "bnj,bij->bni", own_blocks, first, preferred_element_type=jnp.float32
            )
            remote_part = jnp.einsum(
                "bnj,bij->bni", other_blocks, second, preferred_element_type=jnp.float32
            )
            return (local_part + remote_part).astype(jnp.bfloat16)

        result = lax.map(
            one_group,
            (
                field.reshape((group_total, group_size) + field.shape[1:]),
                partner.reshape((group_total, group_size) + partner.shape[1:]),
                chosen.reshape(group_total, group_size, 2),
            ),
        )
        return result.reshape(field.shape)

    field = vectors
    for offset in range(middle_bits):
        partner = partner_2(field, "gy", offset)
        field = apply_level(field, partner, factor_index, offset)
    for offset in range(high_bits):
        partner = partner_2(field, "gx", offset)
        field = apply_level(field, partner, factor_index, middle_bits + offset)
    return field


def solution(mesh):
    placed = (P(("gx", "gy"), None, None), P(), P(("gx", "gy"), None, None), P())
    return jax.shard_map(
        body, mesh=mesh, in_specs=placed, out_specs=P(("gx", "gy"), None, None), check_vma=False
    )
```

profile of v0, /device:TPU:6, one launch (start us, length us, event | category | flops | bytes accessed | tf_op | source)
XLA Modules:
  0.0 815.8 jit_solution(6807626861065248504)
XLA Ops:
  23.3 58.2 %while.80 = (s32[]{:T(128)}, bf16[4,64,32,128]{3,2,1,0:T(8,128)(2,1)}, bf16[4,64,32,128]{3,2,1,0:T(8,128)(2,1)}, s32[4,64,2]{1,0,2:T(4,128)S(1)}, bf16[16,128,12...) while((s32[]{:T(128)}, bf16[4,64,32,128]{3,2,1,0:T(8,128)(2,1)}, ...), condition=%wide.region_1.3_spmd, body=%wide.region_0.2_spmd.sunk | while | flops 136841984 | bytes 16266065 | solution.py:37
  33.7 4.1 fusion.278
  77.4 4.1 fusion.278
  83.1 46.7 %collective-permute-done.1 = bf16[256,32,128]{2,1,0:T(8,128)(2,1)} collective-permute-done((bf16[256,32,128]{2,1,0:T(8,128)(2,1)}, bf16[256,32,128]{2,1,0:T(8,128)(2,1)}, u32[]{:S(2)}, u32[]{:S(2)}) %collective-permute-start.1) | collective-permute-done | bytes 2097184 | tf_op jit(solution)/shard_map/ppermute | solution.py:10
  131.5 50.1 %while.81 = (s32[]{:T(128)}, bf16[4,64,32,128]{3,2,1,0:T(8,128)(2,1)}, bf16[4,64,32,128]{3,2,1,0:T(8,128)(2,1)}, s32[4,64,2]{1,0,2:T(4,128)S(1)}, bf16[16,128,12...) while((s32[]{:T(128)}, bf16[4,64,32,128]{3,2,1,0:T(8,128)(2,1)}, ...), condition=%wide.region_3.5_spmd, body=%wide.region_2.4_spmd.sunk | while | flops 136841984 | bytes 16266065 | solution.py:37
  139.9 4.1 fusion.284
  165.0 4.1 fusion.284
  184.8 45.7 %collective-permute-done.2 = bf16[256,32,128]{2,1,0:T(8,128)(2,1)} collective-permute-done((bf16[256,32,128]{2,1,0:T(8,128)(2,1)}, bf16[256,32,128]{2,1,0:T(8,128)(2,1)}, u32[]{:S(2)}, u32[]{:S(2)}) %collective-permute-start.2) | collective-permute-done | bytes 2097184 | tf_op jit(solution)/shard_map/ppermute | solution.py:10
  232.3 49.7 %while.82 = (s32[]{:T(128)}, bf16[4,64,32,128]{3,2,1,0:T(8,128)(2,1)}, bf16[4,64,32,128]{3,2,1,0:T(8,128)(2,1)}, s32[4,64,2]{1,0,2:T(4,128)S(1)}, bf16[16,128,12...) while((s32[]{:T(128)}, bf16[4,64,32,128]{3,2,1,0:T(8,128)(2,1)}, ...), condition=%wide.region_5.7_spmd, body=%wide.region_4.6_spmd.sunk | while | flops 136841984 | bytes 16266065 | solution.py:37
  240.6 4.1 fusion.290
  253.0 4.1 fusion.290
  265.4 4.1 fusion.290
  277.8 4.1 fusion.290
  285.3 89.8 %collective-permute-done.3 = bf16[256,32,128]{2,1,0:T(8,128)(2,1)} collective-permute-done((bf16[256,32,128]{2,1,0:T(8,128)(2,1)}, bf16[256,32,128]{2,1,0:T(8,128)(2,1)}, u32[]{:S(2)}, u32[]{:S(2)}) %collective-permute-start.3) | collective-permute-done | bytes 2097184 | tf_op jit(solution)/shard_map/ppermute | solution.py:10
  376.7 44.8 %while.83 = (s32[]{:T(128)}, bf16[4,64,32,128]{3,2,1,0:T(8,128)(2,1)}, bf16[4,64,32,128]{3,2,1,0:T(8,128)(2,1)}, s32[4,64,2]{1,0,2:T(4,128)S(1)}, bf16[16,128,12...) while((s32[]{:T(128)}, bf16[4,64,32,128]{3,2,1,0:T(8,128)(2,1)}, ...), condition=%wide.region_7.9_spmd, body=%wide.region_6.8_spmd.sunk | while | flops 136841984 | bytes 16266065 | solution.py:37
  421.5 6.6 collective-permute-start.4
  428.1 91.1 %collective-permute-done.4 = bf16[256,32,128]{2,1,0:T(8,128)(2,1)} collective-permute-done((bf16[256,32,128]{2,1,0:T(8,128)(2,1)}, bf16[256,32,128]{2,1,0:T(8,128)(2,1)}, u32[]{:S(2)}, u32[]{:S(2)}) %collective-permute-start.4) | collective-permute-done | bytes 2097184 | tf_op jit(solution)/shard_map/ppermute | solution.py:10
  520.9 45.3 %while.84 = (s32[]{:T(128)}, bf16[4,64,32,128]{3,2,1,0:T(8,128)(2,1)}, bf16[4,64,32,128]{3,2,1,0:T(8,128)(2,1)}, s32[4,64,2]{1,0,2:T(4,128)S(1)}, bf16[16,128,12...) while((s32[]{:T(128)}, bf16[4,64,32,128]{3,2,1,0:T(8,128)(2,1)}, ...), condition=%wide.region_9.11_spmd, body=%wide.region_8.10_spmd.sunk | while | flops 136841984 | bytes 16266065 | solution.py:37
  567.1 45.9 %collective-permute-done.5 = bf16[256,32,128]{2,1,0:T(8,128)(2,1)} collective-permute-done((bf16[256,32,128]{2,1,0:T(8,128)(2,1)}, bf16[256,32,128]{2,1,0:T(8,128)(2,1)}, u32[]{:S(2)}, u32[]{:S(2)}) %collective-permute-start.5) | collective-permute-done | bytes 2097184 | tf_op jit(solution)/shard_map/ppermute | solution.py:10
  614.6 35.1 %while.85 = (s32[]{:T(128)}, bf16[4,64,32,128]{3,2,1,0:T(8,128)(2,1)}, bf16[4,64,32,128]{3,2,1,0:T(8,128)(2,1)}, s32[4,64,2]{1,0,2:T(4,128)S(1)}, bf16[16,128,12...) while((s32[]{:T(128)}, bf16[4,64,32,128]{3,2,1,0:T(8,128)(2,1)}, ...), condition=%wide.region_11.13_spmd, body=%wide.region_10.12_spmd.sunk | while | flops 136841984 | bytes 16266065 | solution.py:37
  651.2 45.9 %collective-permute-done.6 = bf16[256,32,128]{2,1,0:T(8,128)(2,1)} collective-permute-done((bf16[256,32,128]{2,1,0:T(8,128)(2,1)}, bf16[256,32,128]{2,1,0:T(8,128)(2,1)}, u32[]{:S(2)}, u32[]{:S(2)}) %collective-permute-start.6) | collective-permute-done | bytes 2097184 | tf_op jit(solution)/shard_map/ppermute | solution.py:10
  698.8 35.1 %while.86 = (s32[]{:T(128)}, bf16[4,64,32,128]{3,2,1,0:T(8,128)(2,1)}, bf16[4,64,32,128]{3,2,1,0:T(8,128)(2,1)}, s32[4,64,2]{1,0,2:T(4,128)S(1)}, bf16[16,128,12...) while((s32[]{:T(128)}, bf16[4,64,32,128]{3,2,1,0:T(8,128)(2,1)}, ...), condition=%wide.region_13.15_spmd, body=%wide.region_12.14_spmd.sunk | while | flops 136841984 | bytes 16266065 | solution.py:37
  734.0 45.0 %collective-permute-done.7 = bf16[256,32,128]{2,1,0:T(8,128)(2,1)} collective-permute-done((bf16[256,32,128]{2,1,0:T(8,128)(2,1)}, bf16[256,32,128]{2,1,0:T(8,128)(2,1)}, u32[]{:S(2)}, u32[]{:S(2)}) %collective-permute-start.7) | collective-permute-done | bytes 2097184 | tf_op jit(solution)/shard_map/ppermute | solution.py:10
  780.6 35.1 %while.87 = (s32[]{:T(128)}, bf16[4,64,32,128]{3,2,1,0:T(8,128)(2,1)}, bf16[4,64,32,128]{3,2,1,0:T(8,128)(2,1)}, s32[4,64,2]{1,0,2:T(4,128)S(1)}, bf16[16,128,12...) while((s32[]{:T(128)}, bf16[4,64,32,128]{3,2,1,0:T(8,128)(2,1)}, ...), condition=%wide.region_15.17_spmd, body=%wide.region_14.16_spmd.sunk | while | flops 136841984 | bytes 16266065 | solution.py:37
  (247 shorter events, 350.9 us)
Async XLA Ops:
  0.0 21.6 %collective-permute-start = (bf16[256,32,128]{2,1,0:T(8,128)(2,1)}, bf16[256,32,128]{2,1,0:T(8,128)(2,1)}, u32[]{:S(2)}, u32[]{:S(2)}) collective-permute-start(bf16[256,32,128]{2,1,0:T(8,128)(2,1)} %param.22), channel_id=1, source_target_pairs={{0,1},{1,0},{2,3},{3,2},{4,5},{5,4},{6,7},{7,6},{8,9},{9,8},{10,11... | collective-permute-start | bytes 6291464 | tf_op jit(solution)/shard_map/ppermute | solution.py:10
  81.5 48.4 %collective-permute-start.1 = (bf16[256,32,128]{2,1,0:T(8,128)(2,1)}, bf16[256,32,128]{2,1,0:T(8,128)(2,1)}, u32[]{:S(2)}, u32[]{:S(2)}) collective-permute-start(bf16[256,32,128]{2,1,0:T(8,128)(2,1)} %bitcast.273), channel_id=1, source_target_pairs={{0,2},{1,3},{2,0},{3,1},{4,6},{5,7},{6,4},{7,5},{8,10},{9,11},{10,... | collective-permute-start | bytes 6291464 | tf_op jit(solution)/shard_map/ppermute | solution.py:10
  181.6 49.0 %collective-permute-start.2 = (bf16[256,32,128]{2,1,0:T(8,128)(2,1)}, bf16[256,32,128]{2,1,0:T(8,128)(2,1)}, u32[]{:S(2)}, u32[]{:S(2)}) collective-permute-start(bf16[256,32,128]{2,1,0:T(8,128)(2,1)} %bitcast.274), channel_id=1, source_target_pairs={{0,4},{1,5},{2,6},{3,7},{4,0},{5,1},{6,2},{7,3},{8,12},{9,13},{10,... | collective-permute-start | bytes 6291464 | tf_op jit(solution)/shard_map/ppermute | solution.py:10
  281.9 93.1 %collective-permute-start.3 = (bf16[256,32,128]{2,1,0:T(8,128)(2,1)}, bf16[256,32,128]{2,1,0:T(8,128)(2,1)}, u32[]{:S(2)}, u32[]{:S(2)}) collective-permute-start(bf16[256,32,128]{2,1,0:T(8,128)(2,1)} %bitcast.275), channel_id=1, source_target_pairs={{0,8},{1,9},{2,10},{3,11},{4,12},{5,13},{6,14},{7,15},{8,0},{9,1},... | collective-permute-start | bytes 6291464 | tf_op jit(solution)/shard_map/ppermute | solution.py:10
  421.5 97.8 %collective-permute-start.4 = (bf16[256,32,128]{2,1,0:T(8,128)(2,1)}, bf16[256,32,128]{2,1,0:T(8,128)(2,1)}, u32[]{:S(2)}, u32[]{:S(2)}) collective-permute-start(bf16[256,32,128]{2,1,0:T(8,128)(2,1)} %bitcast.276), channel_id=1, source_target_pairs={{0,16},{1,17},{2,18},{3,19},{4,20},{5,21},{6,22},{7,23},{8,24},{9,... | collective-permute-start | bytes 6291464 | tf_op jit(solution)/shard_map/ppermute | solution.py:10
  566.2 46.8 %collective-permute-start.5 = (bf16[256,32,128]{2,1,0:T(8,128)(2,1)}, bf16[256,32,128]{2,1,0:T(8,128)(2,1)}, u32[]{:S(2)}, u32[]{:S(2)}) collective-permute-start(bf16[256,32,128]{2,1,0:T(8,128)(2,1)} %bitcast.277), channel_id=1, source_target_pairs={{0,32},{32,0},{64,96},{96,64},{128,160},{160,128},{192,224},{224,1... | collective-permute-start | bytes 6291464 | tf_op jit(solution)/shard_map/ppermute | solution.py:10
  649.7 47.4 %collective-permute-start.6 = (bf16[256,32,128]{2,1,0:T(8,128)(2,1)}, bf16[256,32,128]{2,1,0:T(8,128)(2,1)}, u32[]{:S(2)}, u32[]{:S(2)}) collective-permute-start(bf16[256,32,128]{2,1,0:T(8,128)(2,1)} %bitcast.278), channel_id=1, source_target_pairs={{0,64},{32,96},{64,0},{96,32},{128,192},{160,224},{192,128},{224,1... | collective-permute-start | bytes 6291464 | tf_op jit(solution)/shard_map/ppermute | solution.py:10
  698.8 35.1 %copy-start.1 = (s32[256,1,2]{0,2,1:T(2,128)S(1)}, s32[256,1,2]{0,2,1:T(2,128)}, u32[]{:S(2)}) copy-start(s32[256,1,2]{0,2,1:T(2,128)} %get-tuple-element.486) | copy-start | bytes 6148
  733.9 46.7 %copy-start = (bf16[16,128,128]{2,1,0:T(8,128)(2,1)S(1)}, bf16[16,128,128]{2,1,0:T(8,128)(2,1)}, u32[]{:S(2)}) copy-start(bf16[16,128,128]{2,1,0:T(8,128)(2,1)} %get-tuple-element.1045) | copy-start | bytes 1572868
  733.9 45.1 %collective-permute-start.7 = (bf16[256,32,128]{2,1,0:T(8,128)(2,1)}, bf16[256,32,128]{2,1,0:T(8,128)(2,1)}, u32[]{:S(2)}, u32[]{:S(2)}) collective-permute-start(bf16[256,32,128]{2,1,0:T(8,128)(2,1)} %bitcast.279), channel_id=1, source_target_pairs={{0,128},{32,160},{64,192},{96,224},{128,0},{160,32},{192,64},{224,... | collective-permute-start | bytes 6291464 | tf_op jit(solution)/shard_map/ppermute | solution.py:10
where the time goes:
time: 818 us; the launch traced here: 816 us
  waiting for transfers between devices  410 us (50%)
  matrix products  234 us (29%)
  local copies, waits for them, and re-layouts  138 us (17%)
  starting transfers between devices  16.8 us (2%)
  between operations  14.9 us (2%)
    ppermute x8, waiting for transfers between devices, partner_2(): lax.ppermute(array, axis, [(i, i ^ 1 << distance) for i in range(lax.axis...  410 us
    dot_general x32, matrix products, one_group(): jnp.einsum('bnj,bij->bni', own_blocks, first, preferred_element_type=jnp....  122 us
    dot_general x32, matrix products, one_group(): jnp.einsum('bnj,bij->bni', other_blocks, second, preferred_element_type=j...  113 us
    gather x32, local copies, waits for them, and re-layouts, one_group(): first = jnp.take(level_table, selected[:, 0], axis=0)  58.9 us
    gather x32, local copies, waits for them, and re-layouts, one_group(): second = jnp.take(level_table, selected[:, 1], axis=0)  58.8 us
    ppermute x8, starting transfers between devices, partner_2(): lax.ppermute(array, axis, [(i, i ^ 1 << distance) for i in range(lax.axis...  16.8 us
  transfers between devices with their start and end apart: 8, of which 7 were waited for; matrix products, arithmetic and copies ran while one was open for 1% of the time, Pallas kernels for 0%

commit v1 on v0

v1 whole, which is shorter than its diff:
```python
import functools

import jax
import jax.numpy as jnp
from jax import lax
from jax.experimental import pallas as pl
from jax.experimental.pallas import tpu as pltpu
from jax.sharding import PartitionSpec as P

UNROLL = 4


def levels_kernel(levels, order_ref, index_ref, field_ref, table_ref, out_ref):
    blocks, _, rank = field_ref.shape
    out_ref[...] = field_ref[...]
    for level in range(levels):
        slot = order_ref[level]

        def step(i, carry, level=level, slot=slot):
            done = []
            for u in range(UNROLL):
                t = i * UNROLL + u
                g = ((t >> level) << (level + 1)) | (t & ((1 << level) - 1))
                p = g | (1 << level)
                at_g, at_p = (g * levels + slot) * 2, (p * levels + slot) * 2
                from_g = jnp.concatenate(
                    [table_ref[slot, index_ref[at_g]], table_ref[slot, index_ref[at_p + 1]]], axis=1
                )
                from_p = jnp.concatenate(
                    [table_ref[slot, index_ref[at_g + 1]], table_ref[slot, index_ref[at_p]]], axis=1
                )
                both = jnp.dot(
                    jnp.concatenate([out_ref[g], out_ref[p]], axis=1),
                    jnp.concatenate([from_g, from_p], axis=0),
                    preferred_element_type=jnp.float32,
                ).astype(jnp.bfloat16)
                done.append((g, p, both))
            for g, p, both in done:
                out_ref[g] = both[:, :rank]
                out_ref[p] = both[:, rank:]
            return carry

        lax.fori_loop(0, blocks // 2 // UNROLL, step, 0)


def body(vectors, coupling_table, factor_index, level_order):
    axes = ("gx", "gy")
    blocks, levels = factor_index.shape[:2]
    field = lax.all_to_all(vectors, axes, 0, 0, tiled=True)
    index = lax.all_to_all(factor_index.reshape(blocks, levels * 2), axes, 0, 0, tiled=True)
    smem, vmem = pl.BlockSpec(memory_space=pltpu.SMEM), pl.BlockSpec(memory_space=pltpu.VMEM)
    field = pl.pallas_call(
        functools.partial(levels_kernel, levels),
        out_shape=jax.ShapeDtypeStruct(field.shape, field.dtype),
        in_specs=[smem, smem, vmem, vmem],
        out_specs=vmem,
        compiler_params=pltpu.CompilerParams(vmem_limit_bytes=40 << 20),
    )(level_order, index.reshape(-1), field, jnp.swapaxes(coupling_table, 2, 3))
    return lax.all_to_all(field, axes, 0, 0, tiled=True)


def solution(mesh):
    placed = (P(("gx", "gy"), None, None), P(), P(("gx", "gy"), None, None), P())
    return jax.shard_map(
        body, mesh=mesh, in_specs=placed, out_specs=P(("gx", "gy"), None, None), check_vma=False
    )
```

time: 818 us -> 204 us (0.25)
  waiting for transfers between devices: 410 us -> 44.3 us
  matrix products: 234 us -> 0 us
  local copies, waits for them, and re-layouts: 138 us -> 11.4 us
  blocking collectives: 0 us -> 84.9 us
  Pallas kernels: 0 us -> 53.1 us
  between operations: 14.9 us -> 0.05 us
  starting transfers between devices: 16.8 us -> 7.04 us
    ppermute x8 -> x0, waiting for transfers between devices: 410 us -> none  [partner_2(): lax.ppermute(array, axis, [(i, i ^ 1 << distance) for i in range(lax.axis...]
    dot_general x64 -> x0, matrix products: 234 us -> none  [the longest x32 122 us: one_group(): jnp.einsum('bnj,bij->bni', own_blocks, first, preferred_element_type=jnp....]
    gather x64 -> x0, local copies, waits for them, and re-layouts: 118 us -> none  [the longest x32 58.9 us: one_group(): first = jnp.take(level_table, selected[:, 0], axis=0)]
    all_to_all x0 -> x2, blocking collectives: none -> 84.9 us  [the longest x1 58.9 us: body(): return lax.all_to_all(field, axes, 0, 0, tiled=True)]
    pallas_call x0 -> x1, Pallas kernels: none -> 53.1 us  [body(): pl.pallas_call(functools.partial(levels_kernel, levels), out_shape=jax.Sh...]
    all_to_all x0 -> x1, waiting for transfers between devices: none -> 44.3 us  [body(): field = lax.all_to_all(vectors, axes, 0, 0, tiled=True)]
    ppermute x8 -> x0, starting transfers between devices: 16.8 us -> none  [partner_2(): lax.ppermute(array, axis, [(i, i ^ 1 << distance) for i in range(lax.axis...]
    another operation x8 -> x0, local copies, waits for them, and re-layouts: 13.2 us -> none
  transfers between devices with their start and end apart: 8 -> 1, of which waited for: 7 -> 1; matrix products, arithmetic and copies ran while one was open for 1% -> 4% of each run, Pallas kernels for 0% -> 0%
where the time goes in v1:
time: 204 us; the launch traced here: 202 us
  blocking collectives  84.9 us (42%)
  Pallas kernels  53.1 us (26%)
  waiting for transfers between devices  44.3 us (22%)
  local copies, waits for them, and re-layouts  11.4 us (6%)
  starting transfers between devices  7.04 us (3%)
    all_to_all x1, blocking collectives, body(): return lax.all_to_all(field, axes, 0, 0, tiled=True)  58.9 us
    pallas_call x1, Pallas kernels, body(): pl.pallas_call(functools.partial(levels_kernel, levels), out_shape=jax.Sh...  53.1 us
    all_to_all x1, waiting for transfers between devices, body(): field = lax.all_to_all(vectors, axes, 0, 0, tiled=True)  44.3 us
    all_to_all x1, blocking collectives, body(): lax.all_to_all(factor_index.reshape(blocks, levels * 2), axes, 0, 0, tile...  25.9 us
    unnamed x6, local copies, waits for them, and re-layouts  10 us
    all_to_all x1, starting transfers between devices, body(): field = lax.all_to_all(vectors, axes, 0, 0, tiled=True)  7.04 us
  transfers between devices with their start and end apart: 1, of which 1 were waited for; matrix products, arithmetic and copies ran while one was open for 4% of the time, Pallas kernels for 0%

profile of v1, /device:TPU:6, one launch (start us, length us, event | category | flops | bytes accessed | tf_op | source)
XLA Modules:
  0.0 201.8 jit_solution(6527829871873077182)
XLA Ops:
  0.0 0.7 all_to_all.12
  0.7 0.1 copy.10
  0.8 25.9 %all_to_all.19 = s32[256,1,16]{2,1,0:T(1,128)S(1)} all-to-all(s32[256,1,16]{2,1,0:T(1,128)S(1)} %copy.10), channel_id=1, replica_groups=mesh['gx'=8,'gy'=32] {'gx','gy'}, dimensions={0} | all-to-all | bytes 32768 | tf_op jit(solution)/shard_map/all_to_all | solution.py:50
  26.8 7.0 %all-to-all-start.1 = ((bf16[256,32,128]{2,1,0:T(8,128)(2,1)}), bf16[256,32,128]{2,1,0:T(8,128)(2,1)S(1)}, u32[]{:S(2)}, u32[]{:S(2)}) async-start(bf16[256,32,128]{2,1,0:T(8,128)(2,1)} %param.4), calls=%async_computation.1 | async-start | bytes 4194304 | tf_op jit(solution)/shard_map/all_to_all | solution.py:49
  33.8 0.0 copy-start.1
  33.8 6.5 %copy.11 = bf16[8,16,128,128]{2,3,1,0:T(8,128)(2,1)} copy(bf16[8,16,128,128]{3,2,1,0:T(8,128)(2,1)} %param.5) | data formatting | bytes 8388608 | tf_op args[1]
  40.3 0.5 broadcast.3
  40.8 1.0 reduce.3
  41.8 0.1 reshape.8.index_ref
  41.9 44.3 %all-to-all-done.1.field_ref = bf16[256,32,128]{2,1,0:T(8,128)(2,1)S(1)} async-done(((bf16[256,32,128]{2,1,0:T(8,128)(2,1)}), bf16[256,32,128]{2,1,0:T(8,128)(2,1)S(1)}, u32[]{:S(2)}, u32[]{:S(2)}) %all-to-all-start.1) | async-done | bytes 2097184 | tf_op jit(solution)/shard_map/all_to_all | solution.py:49
  86.3 0.0 copy-done.1
  86.3 0.0 copy-start
  86.3 2.2 %copy-done = bf16[8,16,128,128]{2,3,1,0:T(8,128)(2,1)S(1)} copy-done((bf16[8,16,128,128]{2,3,1,0:T(8,128)(2,1)S(1)}, bf16[8,16,128,128]{2,3,1,0:T(8,128)(2,1)}, u32[]{:S(2)}) %copy-start) | copy-done | bytes 4194328
  88.4 53.1 %shard_map.46 = bf16[256,32,128]{2,1,0:T(8,128)(2,1)S(1)} custom-call(s32[8]{0:T(128)S(1)} %copy-done.1, s32[4096]{0:T(1024)S(1)} %reshape.8.index_ref, bf16[256,32,128]{2,1,0:T(8,128)(2,1)S(1)} %all-to-all-done.1.field_ref, bf16[8,16,128,128]{3,2,1,0:T(8,128)(2,1)S(1)} %bitcast.3), custom_call_target="tpu_custom_call" | custom-call | tf_op jit(solution)/shard_map/pallas_call | solution.py:52
  141.6 58.9 %all_to_all.20 = bf16[256,32,128]{2,1,0:T(8,128)(2,1)S(1)} all-to-all(bf16[256,32,128]{2,1,0:T(8,128)(2,1)S(1)} %shard_map.46), channel_id=1, replica_groups=mesh['gx'=8,'gy'=32] {'gx','gy'}, dimensions={0} | all-to-all | bytes 4194304 | tf_op jit(solution)/shard_map/all_to_all | solution.py:59
  200.5 1.3 copy.13
Async XLA Ops:
  26.8 59.5 %all-to-all-start.1 = ((bf16[256,32,128]{2,1,0:T(8,128)(2,1)}), bf16[256,32,128]{2,1,0:T(8,128)(2,1)S(1)}, u32[]{:S(2)}, u32[]{:S(2)}) async-start(bf16[256,32,128]{2,1,0:T(8,128)(2,1)} %param.4), calls=%async_computation.1 | async-start | bytes 4194304 | tf_op jit(solution)/shard_map/all_to_all | solution.py:49
  33.8 52.4 %copy-start.1 = (s32[8]{0:T(128)S(1)}, s32[8]{0:T(128)}, u32[]{:S(2)}) copy-start(s32[8]{0:T(128)} %order_ref.1) | copy-start | bytes 100
  86.3 2.2 %copy-start = (bf16[8,16,128,128]{2,3,1,0:T(8,128)(2,1)S(1)}, bf16[8,16,128,128]{2,3,1,0:T(8,128)(2,1)}, u32[]{:S(2)}) copy-start(bf16[8,16,128,128]{2,3,1,0:T(8,128)(2,1)} %copy.11) | copy-start | bytes 12582916

commit v2 on v1

v2 whole, which is shorter than its diff:
```python
import jax
import jax.numpy as jnp
from jax import lax
from jax.experimental import pallas as pl
from jax.experimental.pallas import tpu as pltpu
from jax.sharding import PartitionSpec as P

MESH = pl.DeviceIdType.MESH
HIGH, MIDDLE = 8, 32
DEVICES = HIGH * MIDDLE
BATCH = 4


def rotated(coordinate, step):
    z, y, core = coordinate // 8, lax.rem(coordinate // 2, 4), lax.rem(coordinate, 2)
    return (
        lax.rem(z + lax.rem(step, 4), 4) * 8
        + lax.rem(y + lax.rem(step // 4, 4), 4) * 2
        + lax.rem(core + step // 16, 2)
    )


def kernel(
    order, index, vectors, table, out,
    field, raw, flat, near, far, chosen,
    table_sem, near_send, near_recv, far_send, far_recv, chosen_sem,
    out_send, out_recv, field_send, field_recv,
):
    gx, gy = lax.axis_index("gx"), lax.axis_index("gy")
    mine = gy * HIGH + gx
    here = gx * MIDDLE + gy

    table_copy = pltpu.make_async_copy(table, raw, table_sem)
    table_copy.start()

    barrier = pltpu.get_barrier_semaphore()

    def greet(i, carry):
        to = (lax.rem(gx + i // MIDDLE, HIGH), lax.rem(gy + lax.rem(i, MIDDLE), MIDDLE))
        pl.semaphore_signal(barrier, inc=1, device_id=to, device_id_type=MESH)
        return carry

    lax.fori_loop(1, DEVICES, greet, 0)
    pl.semaphore_wait(barrier, DEVICES - 1)

    def send_index(r, carry):
        to = rotated(gy, r)
        pltpu.make_async_remote_copy(
            index.at[to], near.at[gy], near_send, near_recv, device_id=(gx, to), device_id_type=MESH
        ).start()
        return carry

    def send_group(s):
        to_x = lax.rem(gx + s, HIGH)

        def send(r, carry):
            to_y = rotated(gy, r)
            pltpu.make_async_remote_copy(
                vectors.at[to_y * HIGH + to_x], field.at[here], field_send, field_recv.at[s],
                device_id=(to_x, to_y), device_id_type=MESH,
            ).start()
            return carry

        return send

    own_index = pltpu.make_async_copy(index.at[gy], near.at[gy], near_recv)
    own_index.start()
    lax.fori_loop(1, MIDDLE, send_index, 0)
    pltpu.make_async_copy(vectors.at[mine], field.at[here], field_recv.at[0]).start()
    lax.fori_loop(1, MIDDLE, send_group(0), 0)
    lax.fori_loop(0, MIDDLE, send_group(1), 0)
    pltpu.make_async_copy(index, near, near_recv).wait()

    def send_far(s, carry):
        to = lax.rem(gx + s, HIGH)
        pltpu.make_async_remote_copy(
            near, far.at[gx], far_send, far_recv, device_id=(to, gy), device_id_type=MESH
        ).start()
        return carry

    lax.fori_loop(1, HIGH, send_far, 0)
    pltpu.make_async_copy(near, far.at[gx], far_recv).start()

    def send_rest(s, carry):
        lax.fori_loop(0, MIDDLE, send_group(s), 0)
        return carry

    lax.fori_loop(2, HIGH, send_rest, 0)

    table_copy.wait()

    def turn(i, carry):
        flat[i] = raw[i].T
        return carry

    lax.fori_loop(0, flat.shape[0], turn, 0, unroll=2)
    pltpu.make_async_copy(far, far, far_recv).wait()
    chosen_copy = pltpu.make_async_copy(far, chosen, chosen_sem)
    chosen_copy.start()
    chosen_copy.wait()

    lane = gx * 16

    def pairs(level, work):
        slot = order[level]
        first = slot * 16
        at = lane + slot * 2
        for start in range(0, len(work), BATCH):
            done = []
            for (gx_, gy_), (px_, py_) in work[start:start + BATCH]:
                own, cross = chosen[gx_, gy_, 0, at], chosen[gx_, gy_, 0, at + 1]
                own_p, cross_p = chosen[px_, py_, 0, at], chosen[px_, py_, 0, at + 1]
                g, p = gx_ * MIDDLE + gy_, px_ * MIDDLE + py_
                weights = jnp.concatenate([
                    jnp.concatenate([flat[first + own], flat[first + cross_p]], axis=1),
                    jnp.concatenate([flat[first + cross], flat[first + own_p]], axis=1),
                ], axis=0)
                both = jnp.dot(
                    jnp.concatenate([field[g], field[p]], axis=1), weights,
                    preferred_element_type=jnp.float32,
                ).astype(jnp.bfloat16)
                done.append((g, p, both))
            for g, p, both in done:
                field[g] = both[:, :128]
                field[p] = both[:, 128:]

    def arrived(s, carry):
        x = lax.rem(gx - s + HIGH, HIGH)
        group = field.at[pl.ds(x * MIDDLE, MIDDLE)]
        pltpu.make_async_copy(group, group, field_recv.at[s]).wait()
        for level in range(5):
            half = 1 << level
            pairs(level, [((x, y), (x, y + half)) for y in range(MIDDLE) if not y & half])
        return carry

    lax.fori_loop(0, HIGH, arrived, 0)

    def send_back(r):
        y = rotated(gy, r)

        def send(s, carry):
            x = lax.rem(gx + s, HIGH)
            pltpu.make_async_remote_copy(
                field.at[x * MIDDLE + y], out.at[mine], out_send, out_recv,
                device_id=(x, y), device_id_type=MESH,
            ).start()
            return carry

        return send

    def finish(r):
        y = rotated(gy, r)
        for level in range(5, 8):
            half = 1 << (level - 5)
            pairs(level, [((x, y), (x + half, y)) for x in range(HIGH) if not x & half])

    finish(0)

    def later(r, carry):
        finish(r)

        @pl.when(r == 1)
        def _():
            pltpu.make_async_copy(field.at[here], out.at[mine], out_recv).start()
            lax.fori_loop(1, HIGH, send_back(0), 0)

        @pl.when(r > 1)
        def _():
            lax.fori_loop(0, HIGH, send_back(r - 1), 0)

        return carry

    lax.fori_loop(1, MIDDLE, later, 0)
    lax.fori_loop(0, HIGH, send_back(MIDDLE - 1), 0)

    def drain(ref, sem):
        pltpu.make_async_copy(ref, ref, sem).wait()

    drain(near.at[pl.ds(0, MIDDLE - 1)], near_send)
    drain(far.at[pl.ds(0, HIGH - 1)], far_send)
    drain(field.at[pl.ds(0, DEVICES - 1)], field_send)
    drain(field.at[pl.ds(0, DEVICES - 1)], out_send)
    drain(field, out_recv)


def body(vectors, coupling_table, factor_index, level_order):
    hbm, smem = pl.BlockSpec(memory_space=pl.ANY), pl.BlockSpec(memory_space=pltpu.SMEM)
    rank = vectors.shape[-1]
    dma = pltpu.SemaphoreType.DMA
    return pl.pallas_call(
        kernel,
        out_shape=jax.ShapeDtypeStruct(vectors.shape, vectors.dtype),
        in_specs=[smem, hbm, hbm, hbm],
        out_specs=hbm,
        scratch_shapes=[
            pltpu.VMEM(vectors.shape, jnp.bfloat16),
            pltpu.VMEM((128, rank, rank), jnp.bfloat16),
            pltpu.VMEM((128, rank, rank), jnp.bfloat16),
            pltpu.VMEM((MIDDLE, 1, 128), jnp.int32),
            pltpu.VMEM((HIGH, MIDDLE, 1, 128), jnp.int32),
            pltpu.SMEM((HIGH, MIDDLE, 1, 128), jnp.int32),
            dma, dma, dma, dma, dma, dma, dma, dma, dma, dma((HIGH,)),
        ],
        compiler_params=pltpu.CompilerParams(
            collective_id=0, has_side_effects=True, vmem_limit_bytes=32 << 20
        ),
    )(level_order, factor_index.reshape(MIDDLE, 1, 128), vectors, coupling_table.reshape(128, rank, rank))


def solution(mesh):
    placed = (P(("gx", "gy"), None, None), P(), P(("gx", "gy"), None, None), P())
    return jax.shard_map(
        body, mesh=mesh, in_specs=placed, out_specs=P(("gx", "gy"), None, None), check_vma=False
    )
```

time: 204 us -> 128 us (0.63)
  blocking collectives: 84.9 us -> 0 us
  Pallas kernels: 53.1 us -> 122 us
  waiting for transfers between devices: 44.3 us -> 0 us
  starting transfers between devices: 7.04 us -> 0 us
  local copies, waits for them, and re-layouts: 11.4 us -> 5.28 us
    all_to_all x2 -> x0, blocking collectives: 84.9 us -> none  [the longest x1 58.9 us: body(): return lax.all_to_all(field, axes, 0, 0, tiled=True)]
    pallas_call x1, Pallas kernels: 53.1 us -> 122 us  [body(): pl.pallas_call(kernel, out_shape=jax.ShapeDtypeStruct(vectors.shape, vect...]
    all_to_all x1 -> x0, waiting for transfers between devices: 44.3 us -> none  [body(): field = lax.all_to_all(vectors, axes, 0, 0, tiled=True)]
    all_to_all x1 -> x0, starting transfers between devices: 7.04 us -> none  [body(): field = lax.all_to_all(vectors, axes, 0, 0, tiled=True)]
    unnamed x6 -> x8, local copies, waits for them, and re-layouts: 10 us -> 4.82 us
  transfers between devices with their start and end apart: 1 -> 0, of which waited for: 1 -> 0; matrix products, arithmetic and copies ran while one was open for 4% -> 0% of each run, Pallas kernels for 0% -> 0%
where the time goes in v2:
time: 128 us; the launch traced here: 127 us
  Pallas kernels  122 us (95%)
  local copies, waits for them, and re-layouts  5.28 us (4%)
    pallas_call x1, Pallas kernels, body(): pl.pallas_call(kernel, out_shape=jax.ShapeDtypeStruct(vectors.shape, vect...  122 us
    unnamed x8, local copies, waits for them, and re-layouts  4.82 us

profile of v2, /device:TPU:6, one launch (start us, length us, event | category | flops | bytes accessed | tf_op | source)
XLA Modules:
  0.0 126.9 jit_solution(930795450851945211)
XLA Ops:
  0.0 0.0 copy-start.2
  0.0 0.0 copy-start.1
  0.0 1.3 %copy.6 = s32[256,8,2]{2,1,0:T(8,128)S(1)} copy(s32[256,8,2]{0,2,1:T(2,128)} %param.6) | data formatting | bytes 32768 | tf_op args[2]
  1.3 0.5 reshape.6
  1.8 0.0 copy-done.2
  1.8 0.0 copy-done.1
  1.8 0.0 copy-start
  1.8 2.2 %copy-done = bf16[8,16,128,128]{3,2,1,0:T(8,128)(2,1)S(1)} copy-done((bf16[8,16,128,128]{3,2,1,0:T(8,128)(2,1)S(1)}, bf16[8,16,128,128]{3,2,1,0:T(8,128)(2,1)}, u32[]{:S(2)}) %copy-start) | copy-done | bytes 4194328
  4.0 121.5 %shard_map.46 = bf16[256,32,128]{2,1,0:T(8,128)(2,1)S(1)} custom-call(s32[8]{0:T(128)S(1)} %copy-done.2, s32[32,1,128]{2,1,0:T(1,128)S(1)} %bitcast.3, bf16[256,32,128]{2,1,0:T(8,128)(2,1)S(1)} %copy-done.1, bf16[128,128,128]{2,1,0:T(8,128)(2,1)S(1)} %bitcast.2), custom_call_target="tpu_custom_call" | custom-call | tf_op jit(solution)/shard_map/pallas_call | solution.py:190
  125.5 1.3 %copy.9 = bf16[256,32,128]{2,1,0:T(8,128)(2,1)} copy(bf16[256,32,128]{2,1,0:T(8,128)(2,1)S(1)} %shard_map.46) | data formatting | bytes 4194304
Async XLA Ops:
  0.0 1.8 %copy-start.2 = (s32[8]{0:T(128)S(1)}, s32[8]{0:T(128)}, u32[]{:S(2)}) copy-start(s32[8]{0:T(128)} %order.1) | copy-start | bytes 100
  0.0 1.8 %copy-start.1 = (bf16[256,32,128]{2,1,0:T(8,128)(2,1)S(1)}, bf16[256,32,128]{2,1,0:T(8,128)(2,1)}, u32[]{:S(2)}) copy-start(bf16[256,32,128]{2,1,0:T(8,128)(2,1)} %vectors.1) | copy-start | bytes 6291460
  1.8 2.2 %copy-start = (bf16[8,16,128,128]{3,2,1,0:T(8,128)(2,1)S(1)}, bf16[8,16,128,128]{3,2,1,0:T(8,128)(2,1)}, u32[]{:S(2)}) copy-start(bf16[8,16,128,128]{3,2,1,0:T(8,128)(2,1)} %param.5) | copy-start | bytes 12582916

commit v3 on v2

--- a/solution.py
+++ b/solution.py
@@ -24,7 +24,7 @@
     order, index, vectors, table, out,
     field, raw, flat, near, far, chosen,
     table_sem, near_send, near_recv, far_send, far_recv, chosen_sem,
-    out_send, out_recv, field_send, field_recv,
+    out_send, out_recv, field_send, field_recv, row_in,
 ):
     gx, gy = lax.axis_index("gx"), lax.axis_index("gy")
     mine = gy * HIGH + gx
@@ -35,13 +35,25 @@
 
     barrier = pltpu.get_barrier_semaphore()
 
-    def greet(i, carry):
-        to = (lax.rem(gx + i // MIDDLE, HIGH), lax.rem(gy + lax.rem(i, MIDDLE), MIDDLE))
+    def greet_row(i, carry):
+        to = (gx, lax.rem(gy + i, MIDDLE))
         pl.semaphore_signal(barrier, inc=1, device_id=to, device_id_type=MESH)
         return carry
 
-    lax.fori_loop(1, DEVICES, greet, 0)
-    pl.semaphore_wait(barrier, DEVICES - 1)
+    def greet_column(i, carry):
+        to = (lax.rem(gx + i, HIGH), gy)
+        pl.semaphore_signal(barrier, inc=1, device_id=to, device_id_type=MESH)
+        return carry
+
+    def row_is_in(i, carry):
+        to = (lax.rem(gx + i, HIGH), gy)
+        pl.semaphore_signal(row_in.at[gx], inc=1, device_id=to, device_id_type=MESH)
+        return carry
+
+    lax.fori_loop(1, MIDDLE, greet_row, 0)
+    lax.fori_loop(1, HIGH, greet_column, 0)
+    pl.semaphore_wait(barrier, MIDDLE + HIGH - 2)
+    lax.fori_loop(1, HIGH, row_is_in, 0)
 
     def send_index(r, carry):
         to = rotated(gy, r)
@@ -50,25 +62,35 @@
         ).start()
         return carry
 
-    def send_group(s):
+    z, y, core = gy // 8, lax.rem(gy // 2, 4), lax.rem(gy, 2)
+    z_to = [lax.rem(z + i, 4) * 8 for i in range(4)]
+    y_to = [lax.rem(y + i, 4) * 2 for i in range(4)]
+
+    def send_group(s, half, skip=0):
         to_x = lax.rem(gx + s, HIGH)
-
-        def send(r, carry):
-            to_y = rotated(gy, r)
+        for i in range(skip, 16):
+            to_y = z_to[i % 4] + y_to[i // 4] + half
             pltpu.make_async_remote_copy(
                 vectors.at[to_y * HIGH + to_x], field.at[here], field_send, field_recv.at[s],
                 device_id=(to_x, to_y), device_id_type=MESH,
             ).start()
-            return carry
-
-        return send
 
     own_index = pltpu.make_async_copy(index.at[gy], near.at[gy], near_recv)
     own_index.start()
     lax.fori_loop(1, MIDDLE, send_index, 0)
     pltpu.make_async_copy(vectors.at[mine], field.at[here], field_recv.at[0]).start()
-    lax.fori_loop(1, MIDDLE, send_group(0), 0)
-    lax.fori_loop(0, MIDDLE, send_group(1), 0)
+    send_group(0, 0, 1)
+
+    @pl.when(core == 1)
+    def _():
+        to = z_to[0] + y_to[0]
+        pltpu.make_async_remote_copy(
+            vectors.at[to * HIGH + gx], field.at[here], field_send, field_recv.at[0],
+            device_id=(gx, to), device_id_type=MESH,
+        ).start()
+
+    pl.semaphore_wait(row_in.at[lax.rem(gx + 1, HIGH)], 1)
+    send_group(1, 0)
     pltpu.make_async_copy(index, near, near_recv).wait()
 
     def send_far(s, carry):
@@ -82,10 +104,27 @@
     pltpu.make_async_copy(near, far.at[gx], far_recv).start()
 
     def send_rest(s, carry):
-        lax.fori_loop(0, MIDDLE, send_group(s), 0)
+        pl.semaphore_wait(row_in.at[lax.rem(gx + s, HIGH)], 1)
+        send_group(s, 0)
         return carry
 
     lax.fori_loop(2, HIGH, send_rest, 0)
+
+    send_group(0, 1, 1)
+
+    @pl.when(core == 0)
+    def _():
+        to = z_to[0] + y_to[0] + 1
+        pltpu.make_async_remote_copy(
+            vectors.at[to * HIGH + gx], field.at[here], field_send, field_recv.at[0],
+            device_id=(gx, to), device_id_type=MESH,
+        ).start()
+
+    def send_second(s, carry):
+        send_group(s, 1)
+        return carry
+
+    lax.fori_loop(1, HIGH, send_second, 0)
 
     table_copy.wait()
 
@@ -184,14 +223,14 @@
 
 
 def body(vectors, coupling_table, factor_index, level_order):
-    hbm, smem = pl.BlockSpec(memory_space=pl.ANY), pl.BlockSpec(memory_space=pltpu.SMEM)
+    hbm, smem = pl.BlockSpec(memory_space=pltpu.HBM), pl.BlockSpec(memory_space=pltpu.SMEM)
     rank = vectors.shape[-1]
     dma = pltpu.SemaphoreType.DMA
     return pl.pallas_call(
         kernel,
         out_shape=jax.ShapeDtypeStruct(vectors.shape, vectors.dtype),
-        in_specs=[smem, hbm, hbm, hbm],
-        out_specs=hbm,
+        in_specs=[smem, pl.BlockSpec(memory_space=pl.ANY), hbm, hbm],
+        out_specs=pl.BlockSpec(memory_space=pl.ANY),
         scratch_shapes=[
             pltpu.VMEM(vectors.shape, jnp.bfloat16),
             pltpu.VMEM((128, rank, rank), jnp.bfloat16),
@@ -200,6 +239,7 @@
             pltpu.VMEM((HIGH, MIDDLE, 1, 128), jnp.int32),
             pltpu.SMEM((HIGH, MIDDLE, 1, 128), jnp.int32),
             dma, dma, dma, dma, dma, dma, dma, dma, dma, dma((HIGH,)),
+            pltpu.SemaphoreType.REGULAR((HIGH,)),
         ],
         compiler_params=pltpu.CompilerParams(
             collective_id=0, has_side_effects=True, vmem_limit_bytes=32 << 20

time: 128 us -> 114 us (0.89)
  Pallas kernels: 122 us -> 107 us
    pallas_call x1, Pallas kernels: 122 us -> 107 us  [body(): pl.pallas_call(kernel, out_shape=jax.ShapeDtypeStruct(vectors.shape, vect...]
where the time goes in v3:
time: 114 us; the launch traced here: 112 us
  Pallas kernels  107 us (94%)
  local copies, waits for them, and re-layouts  5.28 us (5%)
    pallas_call x1, Pallas kernels, body(): pl.pallas_call(kernel, out_shape=jax.ShapeDtypeStruct(vectors.shape, vect...  107 us
    unnamed x8, local copies, waits for them, and re-layouts  4.82 us

profile of v3, /device:TPU:6, one launch (start us, length us, event | category | flops | bytes accessed | tf_op | source)
XLA Modules:
  0.0 112.2 jit_solution(18435608183134096589)
XLA Ops:
  0.0 0.0 copy-start.2
  0.0 0.0 copy-start.1
  0.0 1.3 %copy.6 = s32[256,8,2]{2,1,0:T(8,128)S(1)} copy(s32[256,8,2]{0,2,1:T(2,128)} %param.6) | data formatting | bytes 32768 | tf_op args[2]
  1.3 0.5 reshape.6
  1.8 0.0 copy-done.2
  1.8 0.0 copy-done.1
  1.8 0.0 copy-start
  1.8 2.2 %copy-done = bf16[8,16,128,128]{3,2,1,0:T(8,128)(2,1)S(1)} copy-done((bf16[8,16,128,128]{3,2,1,0:T(8,128)(2,1)S(1)}, bf16[8,16,128,128]{3,2,1,0:T(8,128)(2,1)}, u32[]{:S(2)}) %copy-start) | copy-done | bytes 4194328
  4.0 106.9 %shard_map.46 = bf16[256,32,128]{2,1,0:T(8,128)(2,1)S(1)} custom-call(s32[8]{0:T(128)S(1)} %copy-done.2, s32[32,1,128]{2,1,0:T(1,128)S(1)} %bitcast.3, bf16[256,32,128]{2,1,0:T(8,128)(2,1)S(1)} %copy-done.1, bf16[128,128,128]{2,1,0:T(8,128)(2,1)S(1)} %bitcast.2), custom_call_target="tpu_custom_call" | custom-call | tf_op jit(solution)/shard_map/pallas_call | solution.py:229
  110.9 1.3 %copy.9 = bf16[256,32,128]{2,1,0:T(8,128)(2,1)} copy(bf16[256,32,128]{2,1,0:T(8,128)(2,1)S(1)} %shard_map.46) | data formatting | bytes 4194304
Async XLA Ops:
  0.0 1.8 %copy-start.2 = (s32[8]{0:T(128)S(1)}, s32[8]{0:T(128)}, u32[]{:S(2)}) copy-start(s32[8]{0:T(128)} %order.1) | copy-start | bytes 100
  0.0 1.8 %copy-start.1 = (bf16[256,32,128]{2,1,0:T(8,128)(2,1)S(1)}, bf16[256,32,128]{2,1,0:T(8,128)(2,1)}, u32[]{:S(2)}) copy-start(bf16[256,32,128]{2,1,0:T(8,128)(2,1)} %vectors.1) | copy-start | bytes 6291460
  1.8 2.2 %copy-start = (bf16[8,16,128,128]{3,2,1,0:T(8,128)(2,1)S(1)}, bf16[8,16,128,128]{3,2,1,0:T(8,128)(2,1)}, u32[]{:S(2)}) copy-start(bf16[8,16,128,128]{3,2,1,0:T(8,128)(2,1)} %param.5) | copy-start | bytes 12582916

commit v4 on v2

v4 whole, which is shorter than its diff:
```python
import jax
import jax.numpy as jnp
from jax import lax
from jax.experimental import pallas as pl
from jax.experimental.pallas import tpu as pltpu
from jax.sharding import PartitionSpec as P

MESH = pl.DeviceIdType.MESH
RING, PLANE = 8, 32
DEVICES = RING * PLANE
BATCH = 4
STEPS = (1, 7, 2, 6, 3, 5, 4, 0)


def step_of(k):
    odd = lax.rem(k, 2)
    return (1 - odd) * (k // 2 + 1) + odd * (8 - (k + 1) // 2 - 4 * (k // 7))


def device(z, q):
    return lax.rem(z, 2) * 4 + q // 8, (z // 2) * 8 + lax.rem(q, 8)


def kernel(
    order, index, vectors, table, out,
    field, raw, flat, near, far, chosen,
    table_sem, near_send, near_recv, far_send, far_recv, chosen_sem,
    out_send, out_recv, field_send, field_recv, plane_in,
):
    gx, gy = lax.axis_index("gx"), lax.axis_index("gy")
    x, y, core = lax.rem(gx, 4), lax.rem(gy // 2, 4), lax.rem(gy, 2)
    z = (gy // 8) * 2 + gx // 4
    q = x * 8 + y * 2 + core
    here = z * PLANE + q

    table_copy = pltpu.make_async_copy(table, raw, table_sem)
    table_copy.start()

    z_to = [lax.rem(z + i, RING) for i in range(RING)]
    x_to = [lax.rem(x + i, 4) for i in range(4)]
    y_to = [lax.rem(y + i, 4) for i in range(4)]
    core_to = [core, 1 - core]

    barrier = pltpu.get_barrier_semaphore()

    def greet(at_z, at_q):
        pl.semaphore_signal(barrier, inc=1, device_id=device(at_z, at_q), device_id_type=MESH)

    for k in STEPS[:-1]:
        greet(z_to[k], q)
    for i in range(1, PLANE):
        greet(z, x_to[i % 4] * 8 + y_to[i // 4 % 4] * 2 + core_to[i // 16])
    pl.semaphore_wait(barrier, RING + PLANE - 2)
    for k in STEPS[:-1]:
        pl.semaphore_signal(
            plane_in.at[z], inc=1, device_id=device(z_to[k], q), device_id_type=MESH
        )

    pltpu.make_async_copy(index.at[z], near.at[z], near_recv).start()
    for k in STEPS[:-1]:
        pltpu.make_async_remote_copy(
            index.at[z_to[k]], near.at[z], near_send, near_recv,
            device_id=device(z_to[k], q), device_id_type=MESH,
        ).start()

    def send_group(k, half):
        at_z = z_to[STEPS[k]]
        for i in range(16):
            if STEPS[k] or i:
                at_q = x_to[i % 4] * 8 + y_to[i // 4] * 2 + half
                pltpu.make_async_remote_copy(
                    vectors.at[at_z * PLANE + at_q], field.at[here], field_send, field_recv.at[k],
                    device_id=device(at_z, at_q), device_id_type=MESH,
                ).start()
        if not STEPS[k]:
            @pl.when(core == 1 - half)
            def _():
                at_q = x * 8 + y * 2 + half
                pltpu.make_async_remote_copy(
                    vectors.at[z * PLANE + at_q], field.at[here], field_send, field_recv.at[k],
                    device_id=device(z, at_q), device_id_type=MESH,
                ).start()

    for k in range(RING):
        if STEPS[k]:
            pl.semaphore_wait(plane_in.at[z_to[STEPS[k]]], 1)
        send_group(k, 0)
        if k == 1:
            pltpu.make_async_copy(near, near, near_recv).wait()
            pltpu.make_async_copy(near.at[:, q // 8], far.at[q], far_recv).start()
            for i in range(1, PLANE):
                at_q = x_to[i % 4] * 8 + y_to[i // 4 % 4] * 2 + core_to[i // 16]
                pltpu.make_async_remote_copy(
                    near.at[:, at_q // 8], far.at[q], far_send, far_recv,
                    device_id=device(z, at_q), device_id_type=MESH,
                ).start()
    pltpu.make_async_copy(vectors.at[here], field.at[here], field_recv.at[RING - 1]).start()
    for k in range(RING):
        send_group(k, 1)

    table_copy.wait()

    def turn(i, carry):
        flat[i] = raw[i].T
        return carry

    lax.fori_loop(0, flat.shape[0], turn, 0, unroll=2)
    pltpu.make_async_copy(far, far, far_recv).wait()
    chosen_copy = pltpu.make_async_copy(far, chosen, chosen_sem)
    chosen_copy.start()
    chosen_copy.wait()

    lane = lax.rem(q, 8) * 16

    def pairs(level, work):
        slot = order[level]
        first = slot * 16
        at = lane + slot * 2
        for start in range(0, len(work), BATCH):
            done = []
            for (gz, gq), (pz, pq) in work[start:start + BATCH]:
                own, cross = chosen[gq, gz, 0, at], chosen[gq, gz, 0, at + 1]
                own_p, cross_p = chosen[pq, pz, 0, at], chosen[pq, pz, 0, at + 1]
                g, p = gz * PLANE + gq, pz * PLANE + pq
                weights = jnp.concatenate([
                    jnp.concatenate([flat[first + own], flat[first + cross_p]], axis=1),
                    jnp.concatenate([flat[first + cross], flat[first + own_p]], axis=1),
                ], axis=0)
                both = jnp.dot(
                    jnp.concatenate([field[g], field[p]], axis=1), weights,
                    preferred_element_type=jnp.float32,
                ).astype(jnp.bfloat16)
                done.append((g, p, both))
            for g, p, both in done:
                field[g] = both[:, :128]
                field[p] = both[:, 128:]

    def arrived(k, carry):
        at_z = lax.rem(z - step_of(k) + RING, RING)
        group = field.at[pl.ds(at_z * PLANE, PLANE)]
        pltpu.make_async_copy(group, group, field_recv.at[k]).wait()
        for level in range(3):
            half = 1 << level
            pairs(level, [((at_z, i), (at_z, i + half)) for i in range(PLANE) if not i & half])
        return carry

    lax.fori_loop(0, RING, arrived, 0)

    def place(r):
        return lax.rem(y + lax.rem(r, 4), 4) * 2 + lax.rem(core + r // 4, 2)

    def finish(r):
        yc = place(r)
        for level, dz, dx in ((3, 2, 0), (4, 4, 0), (5, 0, 1), (6, 0, 2), (7, 1, 0)):
            pairs(level, [
                ((i, j * 8 + yc), (i + dz, (j + dx) * 8 + yc))
                for j in range(4) for i in range(RING) if not (i & dz or j & dx)
            ])

    def send_back(r, skip=0):
        yc = place(r)
        for i in range(skip, 32):
            at_z, at_q = z_to[(0, *STEPS)[i % 8]], x_to[i // 8] * 8 + yc
            pltpu.make_async_remote_copy(
                field.at[at_z * PLANE + at_q], out.at[here], out_send, out_recv,
                device_id=device(at_z, at_q), device_id_type=MESH,
            ).start()

    finish(0)

    def later(r, carry):
        finish(r)

        @pl.when(r == 1)
        def _():
            pltpu.make_async_copy(field.at[here], out.at[here], out_recv).start()
            send_back(0, 1)

        @pl.when(r > 1)
        def _():
            send_back(r - 1)

        return carry

    lax.fori_loop(1, 8, later, 0)
    send_back(7)

    def drain(ref, sem):
        pltpu.make_async_copy(ref, ref, sem).wait()

    drain(near.at[pl.ds(0, RING - 1)], near_send)
    drain(far.at[pl.ds(0, PLANE - 1)], far_send)
    drain(field.at[pl.ds(0, DEVICES - 1)], field_send)
    drain(field.at[pl.ds(0, DEVICES - 1)], out_send)
    drain(field, out_recv)


def body(vectors, coupling_table, factor_index, level_order):
    any_space = pl.BlockSpec(memory_space=pl.ANY)
    rank = vectors.shape[-1]
    dma = pltpu.SemaphoreType.DMA
    return pl.pallas_call(
        kernel,
        out_shape=jax.ShapeDtypeStruct(vectors.shape, vectors.dtype),
        in_specs=[pl.BlockSpec(memory_space=pltpu.SMEM), any_space, any_space, any_space],
        out_specs=any_space,
        scratch_shapes=[
            pltpu.VMEM(vectors.shape, jnp.bfloat16),
            pltpu.VMEM((128, rank, rank), jnp.bfloat16),
            pltpu.VMEM((128, rank, rank), jnp.bfloat16),
            pltpu.VMEM((RING, 4, 1, 128), jnp.int32),
            pltpu.VMEM((PLANE, RING, 1, 128), jnp.int32),
            pltpu.SMEM((PLANE, RING, 1, 128), jnp.int32),
            dma, dma, dma, dma, dma, dma, dma, dma, dma, dma((RING,)),
            pltpu.SemaphoreType.REGULAR((RING,)),
        ],
        compiler_params=pltpu.CompilerParams(
            collective_id=0, has_side_effects=True, vmem_limit_bytes=VMEM_LIMIT
        ),
    )(level_order, factor_index.reshape(RING, 4, 1, 128), vectors, coupling_table.reshape(128, rank, rank))


VMEM_LIMIT = 67043328 - (14 << 20)


def solution(mesh):
    placed = (P(("gx", "gy"), None, None), P(), P(("gx", "gy"), None, None), P())
    return jax.shard_map(
        body, mesh=mesh, in_specs=placed, out_specs=P(("gx", "gy"), None, None), check_vma=False
    )
```

time: 128 us -> 109 us (0.85)
  Pallas kernels: 122 us -> 105 us
  local copies, waits for them, and re-layouts: 5.28 us -> 3.02 us
    pallas_call x1, Pallas kernels: 122 us -> 105 us  [body(): pl.pallas_call(kernel, out_shape=jax.ShapeDtypeStruct(vectors.shape, vect...]
    unnamed x8 -> x4, local copies, waits for them, and re-layouts: 4.82 us -> 2.5 us
where the time goes in v4:
time: 109 us; the launch traced here: 108 us
  Pallas kernels  105 us (96%)
  local copies, waits for them, and re-layouts  3.02 us (3%)
    pallas_call x1, Pallas kernels, body(): pl.pallas_call(kernel, out_shape=jax.ShapeDtypeStruct(vectors.shape, vect...  105 us
    unnamed x4, local copies, waits for them, and re-layouts  2.5 us

profile of v4, /device:TPU:6, one launch (start us, length us, event | category | flops | bytes accessed | tf_op | source)
XLA Modules:
  0.0 108.3 jit_solution(3628740614114497381)
XLA Ops:
  0.0 0.0 copy-start
  0.0 1.2 %copy.6 = s32[256,8,2]{2,1,0:T(8,128)S(1)} copy(s32[256,8,2]{0,2,1:T(2,128)} %param.6) | data formatting | bytes 32768 | tf_op args[2]
  1.2 0.5 reshape.6
  1.7 0.0 copy-done
  1.7 105.3 %shard_map.46 = bf16[256,32,128]{2,1,0:T(8,128)(2,1)S(1)} custom-call(s32[8]{0:T(128)S(1)} %copy-done, s32[8,4,1,128]{3,2,1,0:T(1,128)S(1)} %bitcast.2, bf16[256,32,128]{2,1,0:T(8,128)(2,1)} %vectors.1, bf16[128,128,128]{2,1,0:T(8,128)(2,1)} %bitcast.3), custom_call_target="tpu_custom_call" | custom-call | tf_op jit(solution)/shard_map/pallas_call | solution.py:202
  107.0 1.3 %copy.9 = bf16[256,32,128]{2,1,0:T(8,128)(2,1)} copy(bf16[256,32,128]{2,1,0:T(8,128)(2,1)S(1)} %shard_map.46) | data formatting | bytes 4194304
Async XLA Ops:
  0.0 1.7 %copy-start = (s32[8]{0:T(128)S(1)}, s32[8]{0:T(128)}, u32[]{:S(2)}) copy-start(s32[8]{0:T(128)} %order.1) | copy-start | bytes 100

commit v5 on v4

--- a/solution.py
+++ b/solution.py
@@ -23,8 +23,8 @@
 
 def kernel(
     order, index, vectors, table, out,
-    field, raw, flat, near, far, chosen,
-    table_sem, near_send, near_recv, far_send, far_recv, chosen_sem,
+    field, raw, flat, raw_index, stacked, turned, rows, near, far, chosen,
+    table_sem, index_sem, near_send, near_recv, far_send, far_recv, chosen_sem,
     out_send, out_recv, field_send, field_recv, plane_in,
 ):
     gx, gy = lax.axis_index("gx"), lax.axis_index("gy")
@@ -35,6 +35,8 @@
 
     table_copy = pltpu.make_async_copy(table, raw, table_sem)
     table_copy.start()
+    index_copy = pltpu.make_async_copy(index, raw_index, index_sem)
+    index_copy.start()
 
     z_to = [lax.rem(z + i, RING) for i in range(RING)]
     x_to = [lax.rem(x + i, 4) for i in range(4)]
@@ -50,36 +52,48 @@
         greet(z_to[k], q)
     for i in range(1, PLANE):
         greet(z, x_to[i % 4] * 8 + y_to[i // 4 % 4] * 2 + core_to[i // 16])
+
+    stacked[...] = jnp.zeros_like(stacked)
+    index_copy.wait()
+    for k in range(8):
+        stacked[pl.ds(2 * k, 2), :] = raw_index[k]
+    turned[...] = stacked[...].T
+    packed = turned[pl.ds(0, PLANE, stride=8), :]
+    for e in range(1, 8):
+        packed += pltpu.roll(turned[pl.ds(e, PLANE, stride=8), :], 16 * e, 1)
+    for i in range(PLANE):
+        rows[i // 4, i % 4] = packed[i:i + 1, :]
+
     pl.semaphore_wait(barrier, RING + PLANE - 2)
     for k in STEPS[:-1]:
         pl.semaphore_signal(
             plane_in.at[z], inc=1, device_id=device(z_to[k], q), device_id_type=MESH
         )
 
-    pltpu.make_async_copy(index.at[z], near.at[z], near_recv).start()
+    pltpu.make_async_copy(rows.at[z], near.at[z], near_recv).start()
     for k in STEPS[:-1]:
         pltpu.make_async_remote_copy(
-            index.at[z_to[k]], near.at[z], near_send, near_recv,
+            rows.at[z_to[k]], near.at[z], near_send, near_recv,
             device_id=device(z_to[k], q), device_id_type=MESH,
         ).start()
 
+    def send_one(k, at_q):
+        at_z = z_to[STEPS[k]]
+        pltpu.make_async_remote_copy(
+            vectors.at[at_z * PLANE + at_q], field.at[here], field_send, field_recv.at[k],
+            device_id=device(at_z, at_q), device_id_type=MESH,
+        ).start()
+
     def send_group(k, half):
-        at_z = z_to[STEPS[k]]
-        for i in range(16):
-            if STEPS[k] or i:
-                at_q = x_to[i % 4] * 8 + y_to[i // 4] * 2 + half
-                pltpu.make_async_remote_copy(
-                    vectors.at[at_z * PLANE + at_q], field.at[here], field_send, field_recv.at[k],
-                    device_id=device(at_z, at_q), device_id_type=MESH,
-                ).start()
-        if not STEPS[k]:
-            @pl.when(core == 1 - half)
-            def _():
-                at_q = x * 8 + y * 2 + half
-                pltpu.make_async_remote_copy(
-                    vectors.at[z * PLANE + at_q], field.at[here], field_send, field_recv.at[k],
-                    device_id=device(z, at_q), device_id_type=MESH,
-                ).start()
+        @pl.when(core == 1 - half)
+        def _():
+            send_one(k, x * 8 + y * 2 + half)
+
+        for i in range(1, 16):
+            send_one(k, x_to[i % 4] * 8 + y_to[i // 4] * 2 + half)
+
+    for k in range(RING - 1):
+        send_one(k, q)
 
     for k in range(RING):
         if STEPS[k]:
@@ -159,8 +173,8 @@
 
     def send_back(r, skip=0):
         yc = place(r)
-        for i in range(skip, 32):
-            at_z, at_q = z_to[(0, *STEPS)[i % 8]], x_to[i // 8] * 8 + yc
+        for i in range(32 - skip):
+            at_z, at_q = z_to[STEPS[6 - i // 4]], x_to[3 - i % 4] * 8 + yc
             pltpu.make_async_remote_copy(
                 field.at[at_z * PLANE + at_q], out.at[here], out_send, out_recv,
                 device_id=device(at_z, at_q), device_id_type=MESH,
@@ -208,16 +222,20 @@
             pltpu.VMEM(vectors.shape, jnp.bfloat16),
             pltpu.VMEM((128, rank, rank), jnp.bfloat16),
             pltpu.VMEM((128, rank, rank), jnp.bfloat16),
+            pltpu.VMEM((8, 2, DEVICES), jnp.int32),
+            pltpu.VMEM((128, DEVICES), jnp.int32),
+            pltpu.VMEM((DEVICES, 128), jnp.int32),
+            pltpu.VMEM((RING, 4, 1, 128), jnp.int32),
             pltpu.VMEM((RING, 4, 1, 128), jnp.int32),
             pltpu.VMEM((PLANE, RING, 1, 128), jnp.int32),
             pltpu.SMEM((PLANE, RING, 1, 128), jnp.int32),
-            dma, dma, dma, dma, dma, dma, dma, dma, dma, dma((RING,)),
+            dma, dma, dma, dma, dma, dma, dma, dma, dma, dma, dma((RING,)),
             pltpu.SemaphoreType.REGULAR((RING,)),
         ],
         compiler_params=pltpu.CompilerParams(
             collective_id=0, has_side_effects=True, vmem_limit_bytes=VMEM_LIMIT
         ),
-    )(level_order, factor_index.reshape(RING, 4, 1, 128), vectors, coupling_table.reshape(128, rank, rank))
+    )(level_order, jnp.transpose(factor_index, (1, 2, 0)), vectors, coupling_table.reshape(128, rank, rank))
 
 
 VMEM_LIMIT = 67043328 - (14 << 20)

time: 109 us -> 108 us (level)
    unnamed x4 -> x5, local copies, waits for them, and re-layouts: 2.5 us -> 2.69 us
where the time goes in v5:
time: 108 us; the launch traced here: 107 us
  Pallas kernels  104 us (96%)
  local copies, waits for them, and re-layouts  2.69 us (2%)
    pallas_call x1, Pallas kernels, body(): pl.pallas_call(kernel, out_shape=jax.ShapeDtypeStruct(vectors.shape, vect...  104 us
    unnamed x5, local copies, waits for them, and re-layouts  2.69 us

profile of v5, /device:TPU:6, one launch (start us, length us, event | category | flops | bytes accessed | tf_op | source)
XLA Modules:
  0.0 106.9 jit_solution(14209124363439373588)
XLA Ops:
  0.0 0.0 copy-start
  0.0 0.7 copy-done
  0.7 0.0 copy-start.1
  0.7 0.7 copy-done.1
  1.4 104.2 %shard_map.46 = bf16[256,32,128]{2,1,0:T(8,128)(2,1)S(1)} custom-call(s32[8]{0:T(128)S(1)} %copy-done.1, s32[8,2,256]{2,1,0:T(2,128)S(1)} %bitcast.2, bf16[256,32,128]{2,1,0:T(8,128)(2,1)} %vectors.1, bf16[128,128,128]{2,1,0:T(8,128)(2,1)} %bitcast.3), custom_call_target="tpu_custom_call" | custom-call | tf_op jit(solution)/shard_map/pallas_call | solution.py:216
  105.6 1.3 %copy.6 = bf16[256,32,128]{2,1,0:T(8,128)(2,1)} copy(bf16[256,32,128]{2,1,0:T(8,128)(2,1)S(1)} %shard_map.46) | data formatting | bytes 4194304
Async XLA Ops:
  0.0 0.7 copy-start
  0.7 0.7 copy-start.1
